TPU v7x, 1024 devices: a whole 4x8x16 slice. The times are simulated.
1024 devices in a mesh: seq: 8 (over x, core), grp: 16 (over z), head: 8 (over y).
Axes of the slice: x: 4, y: 8, z: 16, core: 2. Of those that a mesh axis runs over, the one named last changes fastest.
Arguments:
- query_feat: bfloat16 [16, 8, 512, 6144], P('grp', 'seq', None, 'head'), may hold values from -6 to 6
- key_feat: bfloat16 [16, 8, 512, 6144], P('grp', 'seq', None, 'head'), may hold values from -6 to 6
- value_feat: bfloat16 [16, 8, 512, 6144], P('grp', 'seq', None, 'head'), may hold values from -6 to 6
- norm_gain: float32 [6144], P('head'), may hold values from 0.5 to 1.5
Outputs:
- attended: bfloat16 [16, 8, 512, 6144], P('grp', 'seq', None, 'head')
All inputs are finite; a program needn't handle non-finite values.
Results may differ from a plain program's by a relative error of at most 0.0049.
Values sent between devices are 32-bit elements; how exact they have to be, the bound alone decides.
A program may use at most 64 MiB of HBM per device.

v0:
```python
import jax
import jax.numpy as jnp
from jax import lax
from jax.sharding import PartitionSpec as P

DH = 128
BLK = 512


def carried_in(shard, axis, combine, identity):
    count, position = (lax.axis_size(axis), lax.axis_index(axis))
    everything = lax.all_gather(shard, axis)
    start = jnp.broadcast_to(jnp.asarray(identity, shard.dtype), shard.shape)

    def hop(k, before):
        reached = k < position
        new = combine(before, everything[k])
        return jnp.where(reached, new, before)

    return lax.fori_loop(0, count, hop, start)


def add_states(earlier, later):
    return earlier + later


def per_device(query_feat, key_feat, value_feat, norm_gain):
    tokens_here = query_feat.shape[2]
    width = query_feat.shape[3]
    heads_here = width // DH
    nblocks = tokens_here // BLK

    def split(array):
        return array.reshape(nblocks, BLK, heads_here, DH)

    queries = split(query_feat)
    keys_all = split(key_feat)
    values = split(value_feat)
    block_sums = jnp.einsum("bthd,bthe->bhde", keys_all, values, preferred_element_type=jnp.float32)
    local_total = jnp.sum(block_sums, axis=0)
    running = jnp.cumsum(block_sums, axis=0)
    earlier_blocks = jnp.concatenate([jnp.zeros_like(block_sums), running[:-1]], axis=0)
    zero_state = jnp.zeros_like(local_total)
    gathered = lax.all_gather(local_total[None], "seq", axis=0, tiled=True)
    position = lax.axis_index("seq")
    lower = (lax.broadcasted_iota(jnp.int32, (gathered.shape[0],), 0) < position).astype(
        jnp.float32
    )
    within = jnp.einsum("j,jhde->hde", lower, gathered, precision=lax.Precision.HIGHEST)
    group_total = jnp.sum(gathered, axis=0)
    before = carried_in(group_total, "grp", add_states, zero_state)
    incoming = before + within
    starts = (incoming[None] + earlier_blocks).astype(jnp.bfloat16)
    rows = lax.broadcasted_iota(jnp.int32, (BLK, BLK), 0)
    columns = lax.broadcasted_iota(jnp.int32, (BLK, BLK), 1)
    causal = rows >= columns
    scores = jnp.einsum("bthd,bshd->bhts", queries, keys_all, preferred_element_type=jnp.float32)
    weights = jnp.where(causal[None, None], scores, 0.0).astype(jnp.bfloat16)
    mixed = jnp.einsum("bhts,bshe->bthe", weights, values, preferred_element_type=jnp.float32)
    mixed = mixed + jnp.einsum(
        "bthd,bhde->bthe", queries, starts, preferred_element_type=jnp.float32
    )
    meansq = jnp.mean(mixed * mixed, axis=-1, keepdims=True)
    gain = norm_gain.reshape(heads_here, DH)
    result = (mixed * lax.rsqrt(meansq + 1e-05) * gain).astype(jnp.bfloat16)
    return result.reshape(query_feat.shape)


def solution(mesh):
    placed = (
        P("grp", "seq", None, "head"),
        P("grp", "seq", None, "head"),
        P("grp", "seq", None, "head"),
        P("head"),
    )
    return jax.shard_map(
        per_device,
        mesh=mesh,
        in_specs=placed,
        out_specs=P("grp", "seq", None, "head"),
        check_vma=False,
    )
```

profile of v0, /device:TPU:2, one launch (start us, length us, event | category | flops | bytes accessed | tf_op | source)
XLA Modules:
  0.0 184.2 jit_solution(18374718130153587812)
XLA Ops:
  6.5 1.5 copy.19
  9.5 46.2 %all-gather.5.cloned.1.call-done = f32[48,128,128]{2,1,0:T(8,128)} async-done(((f32[6,128,128]{2,1,0:T(8,128)}), f32[48,128,128]{2,1,0:T(8,128)}) %all-gather.5.cloned.1.call-update) | async-done | bytes 3145744 | tf_op jit(solution)/shard_map/all_gather | solution.py:44
  55.7 3.0 %reduce_sum.16 = f32[6,128,128]{2,1,0:T(8,128)} reduce(f32[8,6,128,128]{3,2,1,0:T(8,128)} %bitcast.37, f32[]{:T(128)} %constant.36.clone.1), dimensions={0}, to_apply=%region_0.0 | reduce | flops 688128 | bytes 3538948 | tf_op jit(solution)/shard_map/reduce_sum | solution.py:50
  58.8 2.3 %copy.18 = bf16[1,1,512,768]{2,3,1,0:T(8,128)(2,1)} copy(bf16[1,1,512,768]{3,2,1,0:T(8,128)(2,1)} %param.6) | data formatting | bytes 1572864 | tf_op args[0]
  61.9 4.0 %fusion.1 = f32[1,6,128,128]{3,0,2,1:T(1,128)} fusion(f32[8,6,128,128]{3,2,1,0:T(8,128)S(1)} %bitcast.38, s32[]{:T(128)S(6)} %axis_index.28), kind=kOutput, calls=%fused_computation.3 | convolution fusion | flops 9437192 | bytes 3538948 | tf_op jit(solution)/shard_map/j,jhde->hde/dot_general | solution.py:49
  65.9 83.9 %all-gather.7.cloned.1.call-done = f32[96,128,128]{2,1,0:T(8,128)} async-done(((f32[6,128,128]{2,1,0:T(8,128)}), f32[96,128,128]{2,1,0:T(8,128)}) %all-gather.7.cloned.1.call-update) | async-done | bytes 6291472 | tf_op jit(solution)/shard_map/all_gather | solution.py:12
  149.8 18.5 %while.14 = (s32[]{:T(128)}, f32[6,128,128]{2,1,0:T(8,128)S(1)}, s32[]{:T(128)}, f32[16,6,128,128]{3,2,1,0:T(8,128)}, s32[]{:T(128)}, /*index=5*/s32[]{:T(128)}) while((s32[]{:T(128)}, f32[6,128,128]{2,1,0:T(8,128)S(1)}, s32[]{:T(128)}, f32[16,6,128,128]{3,2,1,0:T(8,128)}, s32[]{:T(128)}, /*index=5*/s32[]{:T(128)}) %tuple.40), condition=%wide.region_2.3_spmd.clone, body=%wide.region_1.0_spmd.clone.sunk | while | flops 294916 | bytes 1179749 | solution.py:20
  149.8 1.2 add_select_fusion.2
  151.0 1.1 add_select_fusion.2
  152.2 1.1 add_select_fusion.2
  153.3 1.1 add_select_fusion.2
  154.5 1.1 add_select_fusion.2
  155.6 1.1 add_select_fusion.2
  156.8 1.1 add_select_fusion.2
  157.9 1.1 add_select_fusion.2
  159.1 1.1 add_select_fusion.2
  160.2 1.1 add_select_fusion.2
  161.4 1.1 add_select_fusion.2
  164.9 1.1 add_select_fusion.2
  166.0 1.1 add_select_fusion.2
  168.4 1.6 fusion.10
  170.0 4.6 %fusion.7 = (f32[512,6]{0,1:T(8,128)S(1)}, f32[6,128,512]{2,1,0:T(8,128)}) fusion(f32[6,128,512]{2,1,0:T(8,128)} %fusion.10, bf16[512,6,128]{0,2,1:T(8,128)(2,1)S(1)} %bitcast.42, pred[512,512]{1,0:T(8,128)(4,1)S(1)} %copy-done.8, bf16[512,6,128]{0,2,1:T(8,128)(2,1)S(1)} %bitcast.44, bf16[512,6,128]{0,2,1:T(8,128)(2,1)S(1)} %bitcast.40), kind=kOutput, calls=%fused_computation.10 | convolution fusion | flops 809628672 | bytes 5779456 | tf_op jit(solution)/shard_map/bhts,bshe->bthe/dot_general | solution.py:59
  174.6 1.6 fusion.9
  176.2 1.2 copy.26
  (32 shorter events, 5.7 us)
Async XLA Ops:
  6.5 1.5 copy-start.7
  6.5 49.2 %all-gather.5.cloned.1.call-start = ((), (), s32[]{:S(2)}) async-start(), calls=%async_computation | async-start | bytes 3538944 | tf_op jit(solution)/shard_map/all_gather | solution.py:44
  8.0 1.4 copy-start.1
  8.3 47.4 %copy-start.3 = (bf16[1,1,512,768]{2,3,1,0:T(8,128)(2,1)}, bf16[1,1,512,768]{2,3,1,0:T(8,128)(2,1)S(1)}, u32[]{:S(2)}) copy-start(bf16[1,1,512,768]{2,3,1,0:T(8,128)(2,1)S(1)} %copy.22) | copy-start | bytes 2359300
  9.5 140.3 %all-gather.7.cloned.1.call-start = ((), (), s32[]{:S(2)}) async-start(), calls=%async_computation.1 | async-start | bytes 6684672 | tf_op jit(solution)/shard_map/all_gather | solution.py:12
  55.7 6.1 %copy-start = (f32[48,128,128]{2,1,0:T(8,128)S(1)}, f32[48,128,128]{2,1,0:T(8,128)}, u32[]{:S(2)}) copy-start(f32[48,128,128]{2,1,0:T(8,128)} %all-gather.5.cloned.1.call-done) | copy-start | bytes 9437188
  149.8 18.6 %copy-start.5 = (bf16[1,1,512,768]{2,3,1,0:T(8,128)(2,1)S(1)}, bf16[1,1,512,768]{2,3,1,0:T(8,128)(2,1)}, u32[]{:S(2)}) copy-start(bf16[1,1,512,768]{2,3,1,0:T(8,128)(2,1)} %copy.18) | copy-start | bytes 2359300
  149.8 18.6 %copy-start.6 = (f32[1,6,128,128]{3,0,2,1:T(1,128)S(1)}, f32[1,6,128,128]{3,0,2,1:T(1,128)}, u32[]{:S(2)}) copy-start(f32[1,6,128,128]{3,0,2,1:T(1,128)} %fusion.1) | copy-start | bytes 1179652
  168.3 1.6 copy-start.2
  168.3 1.6 copy-start.4
  168.3 1.6 copy-start.8
  170.0 4.6 %copy-start.9 = (f32[768]{0:T(1024)S(1)}, f32[768]{0:T(1024)}, u32[]{:S(2)}) copy-start(f32[768]{0:T(1024)} %param.9) | copy-start | bytes 9220
Sparse Core Ops, SparseCore 0:
  10.1 45.6 all-gather.4
  58.9 90.8 all-gather.6
where the time goes:
time: 185 us; the launch traced here: 184 us
  waiting for transfers between devices  130 us (70%)
  other arithmetic  23.6 us (13%)
  between operations  13.5 us (7%)
  matrix products  11.3 us (6%)
  local copies, waits for them, and re-layouts  5.26 us (3%)
    all_gather x1, waiting for transfers between devices, carried_in(): everything = lax.all_gather(shard, axis)  83.9 us
    all_gather x1, waiting for transfers between devices, per_device(): gathered = lax.all_gather(local_total[None], 'seq', axis=0, tiled=True)  46.2 us
    select_n x16, other arithmetic, hop(): return jnp.where(reached, new, before)  18.2 us
    dot_general x1, matrix products, per_device(): jnp.einsum('bhts,bshe->bthe', weights, values, preferred_element_type=jnp...  4.61 us
    unnamed x23, local copies, waits for them, and re-layouts  4.11 us
    dot_general x1, matrix products, per_device(): jnp.einsum('j,jhde->hde', lower, gathered, precision=lax.Precision.HIGHEST)  4.02 us
  transfers between devices with their start and end apart: 2, of which 2 were waited for; matrix products, arithmetic and copies ran while one was open for 4% of the time, Pallas kernels for 0%

commit v1 on v0

v1 whole, which is shorter than its diff:
```python
import jax
import jax.numpy as jnp
from jax import lax
from jax.experimental import pallas as pl
from jax.experimental.pallas import tpu as pltpu
from jax.sharding import PartitionSpec as P

DH = 128
MESH = pl.DeviceIdType.MESH
HPC = 2
PIECE = 8


def take(sem, ref):
    pltpu.make_async_copy(ref, ref, sem).wait()


def body(nx, nz, owners, eps, q_hbm, k_hbm, v_hbm, gain_hbm, out_ref, qb, kb, vb, gain, mixed,
         kv, pk, ts, ra, gs, rz, ez, bz, cs, rf,
         in_sem, gain_sem, sc, rc, sa, rcv_a, s1, r1, s2, r2, s3, r3, s4, r4):
    seq, z = lax.axis_index("seq"), lax.axis_index("grp")
    core, x = lax.rem(seq, 2), seq // 2
    tokens, width = qb.shape
    chunks = width // (HPC * DH)
    half = DH
    slc = half // nx
    pieces = slc // PIECE

    def chip(dx):
        return {"seq": lax.rem(x + dx, nx) * 2 + core}

    def along(dz):
        return {"grp": lax.rem(z + dz, nz)}

    partner = {"seq": x * 2 + 1 - core}

    def remote(src, dst, send, recv, where):
        pltpu.make_async_remote_copy(
            src_ref=src, dst_ref=dst, send_sem=send, recv_sem=recv, device_id=where, device_id_type=MESH
        ).start()

    barrier = pltpu.get_barrier_semaphore()
    for dz in range(1, nz):
        pl.semaphore_signal(barrier, inc=1, device_id=along(dz), device_id_type=MESH)
    for dx in range(1, nx):
        pl.semaphore_signal(barrier, inc=1, device_id=chip(dx), device_id_type=MESH)
    pl.semaphore_signal(barrier, inc=1, device_id=partner, device_id_type=MESH)

    loads = []
    for i, (hbm, buf) in enumerate(((k_hbm, kb), (v_hbm, vb), (q_hbm, qb))):
        for n in range(chunks):
            cols = pl.ds(n * HPC * DH, HPC * DH)
            loads.append(pltpu.make_async_copy(hbm.at[:, cols], buf.at[:, cols], in_sem.at[i, n]))
    for n in range(chunks):
        loads[n].start()
        loads[chunks + n].start()
    for n in range(chunks):
        loads[2 * chunks + n].start()
    gain_load = pltpu.make_async_copy(gain_hbm, gain, gain_sem)
    gain_load.start()

    def head(h):
        return pl.ds(h * DH, DH)

    for n in range(chunks):
        loads[n].wait()
        loads[chunks + n].wait()
        for j in range(HPC):
            h = n * HPC + j
            kv[n, pl.ds(j * DH, DH), :] = lax.dot_general(
                kb[:, head(h)], vb[:, head(h)], (((0,), (0,)), ((), ())), preferred_element_type=jnp.float32
            )
        if n == 0:
            pl.semaphore_wait(barrier, nz - 1 + nx - 1 + 1)
        remote(kv.at[n], pk.at[n], sc.at[n], rc.at[n], partner)

    mine = pl.ds(core * half, half)
    for n in range(chunks):
        take(rc.at[n], pk.at[n])
        ts[n] = kv[n, mine, :] + pk[n, mine, :]
        for dx in (2, 1, 3):
            to = lax.rem(x + dx, nx)
            remote(ts.at[n, pl.ds(to * slc, slc)], ra.at[n, pl.ds(x * slc, slc)], sa.at[n], rcv_a.at[n], chip(dx))
        ra[n, pl.ds(x * slc, slc), :] = ts[n, pl.ds(x * slc, slc), :]

    for n in range(chunks):
        take(rcv_a.at[n], ra.at[n, pl.ds(0, (nx - 1) * slc)])
        total = ra[n, pl.ds(0, slc), :]
        for i in range(1, nx):
            total = total + ra[n, pl.ds(i * slc, slc), :]
        gs[n] = total
        for p in range(pieces):
            own = owners[n][p]

            @pl.when(z != own)
            def _():
                remote(gs.at[n, pl.ds(p * PIECE, PIECE)], rz.at[z], s1.at[n], r1, {"grp": own})

            @pl.when(z == own)
            def _():
                rz[own] = gs[n, pl.ds(p * PIECE, PIECE), :]

    rows = tokens // 2
    later = lax.broadcasted_iota(jnp.int32, (rows, rows), 0) >= lax.broadcasted_iota(jnp.int32, (rows, rows), 1)

    def local_attention(h):
        cut = head(h)
        for r in range(2):
            part = pl.ds(r * rows, rows)
            qr = qb[part, cut]
            own_scores = lax.dot_general(qr, kb[part, cut], (((1,), (1,)), ((), ())), preferred_element_type=jnp.float32)
            weights = jnp.where(later, own_scores, 0.0).astype(jnp.bfloat16)
            acc = jnp.dot(weights, vb[part, cut], preferred_element_type=jnp.float32)
            if r == 1:
                first = pl.ds(0, rows)
                full = lax.dot_general(qr, kb[first, cut], (((1,), (1,)), ((), ())), preferred_element_type=jnp.float32)
                acc = acc + jnp.dot(full.astype(jnp.bfloat16), vb[first, cut], preferred_element_type=jnp.float32)
            mixed[part, cut] = acc

    for n in range(chunks):
        loads[2 * chunks + n].wait()
    gain_load.wait()
    heads_here = chunks * HPC
    for h in range(heads_here // 2):
        local_attention(h)

    far_first = sorted(range(1, nz), key=lambda d: -min(d, nz - d))
    for n in range(chunks):
        for p in range(pieces):
            own = owners[n][p]

            @pl.when(z == own)
            def _():
                take(r1, rz.at[pl.ds(0, nz - 1)])
                before = jnp.zeros((PIECE, DH), jnp.float32)
                for i in range(nz):
                    ez[i] = before
                    before = before + rz[i]
                for dz in far_first:
                    to = (own + dz) % nz
                    remote(ez.at[to], bz.at[n, pl.ds(p * PIECE, PIECE)], s2, r2.at[n], {"grp": to})
                bz[n, pl.ds(p * PIECE, PIECE), :] = ez[own]

    for h in range(heads_here // 2, heads_here):
        local_attention(h)

    def owns(n):
        hit = z == owners[n][0]
        for p in range(1, pieces):
            hit = jnp.logical_or(hit, z == owners[n][p])
        return hit

    for n in range(chunks):
        @pl.when(owns(n))
        def _():
            take(r2.at[n], bz.at[n, pl.ds(0, (pieces - 1) * PIECE)])

        @pl.when(jnp.logical_not(owns(n)))
        def _():
            take(r2.at[n], bz.at[n])

        before = bz[n]
        for i in range(nx):
            cs[n, pl.ds(i * slc, slc), :] = before
            before = before + ra[n, pl.ds(i * slc, slc), :]
        land = pl.ds(core * half + x * slc, slc)
        for dx in (2, 1, 3):
            to = lax.rem(x + dx, nx)
            remote(cs.at[n, pl.ds(to * slc, slc)], rf.at[n, land], s3.at[n], r3.at[n], chip(dx))
        rf[n, land, :] = cs[n, pl.ds(x * slc, slc), :]

    for n in range(chunks):
        take(r3.at[n], rf.at[n, pl.ds(0, (nx - 1) * slc)])
        remote(rf.at[n, mine], rf.at[n, mine], s4.at[n], r4.at[n], partner)

    second = core == 1
    for n in range(chunks):
        take(r4.at[n], rf.at[n, pl.ds(0, half)])
        for j in range(HPC):
            h = n * HPC + j
            at = pl.ds(j * DH, DH)
            state = rf[n, at, :] + jnp.where(second, pk[n, at, :], 0.0)
            m = mixed[:, head(h)] + jnp.dot(
                qb[:, head(h)], state.astype(jnp.bfloat16), preferred_element_type=jnp.float32
            )
            meansq = jnp.mean(m * m, axis=-1, keepdims=True)
            out_ref[:, head(h)] = (m * lax.rsqrt(meansq + eps) * gain[head(h)].reshape(1, DH)).astype(jnp.bfloat16)

    for n in range(chunks):
        take(sc.at[n], kv.at[n])
        take(sa.at[n], ts.at[n, pl.ds(0, (nx - 1) * slc)])
        take(s3.at[n], cs.at[n, pl.ds(0, (nx - 1) * slc)])
        take(s4.at[n], rf.at[n, pl.ds(0, half)])

        @pl.when(owns(n))
        def _():
            take(s1.at[n], gs.at[n, pl.ds(0, (pieces - 1) * PIECE)])
            take(s2, ez.at[pl.ds(0, nz - 1)])

        @pl.when(jnp.logical_not(owns(n)))
        def _():
            take(s1.at[n], gs.at[n])


def per_device(query_feat, key_feat, value_feat, norm_gain):
    tokens, width = query_feat.shape[2:]
    nx, nz = lax.axis_size("seq") // 2, lax.axis_size("grp")
    chunks = width // (HPC * DH)
    pieces = DH // nx // PIECE
    owners = [[(n + nz // pieces * p) % nz for p in range(pieces)] for n in range(chunks)]
    half, slc = DH, DH // nx
    f32 = jnp.float32
    dma = pltpu.SemaphoreType.DMA

    def kernel(*refs):
        body(nx, nz, owners, 1e-05, *refs)

    hbm = pl.BlockSpec(memory_space=pltpu.HBM)
    vmem = pl.BlockSpec(memory_space=pltpu.VMEM)
    out = pl.pallas_call(
        kernel,
        out_shape=jax.ShapeDtypeStruct((tokens, width), jnp.bfloat16),
        in_specs=[hbm, hbm, hbm, hbm],
        out_specs=vmem,
        scratch_shapes=[
            pltpu.VMEM((tokens, width), jnp.bfloat16),
            pltpu.VMEM((tokens, width), jnp.bfloat16),
            pltpu.VMEM((tokens, width), jnp.bfloat16),
            pltpu.VMEM((width,), f32),
            pltpu.VMEM((tokens, width), f32),
            pltpu.VMEM((chunks, HPC * DH, DH), f32),
            pltpu.VMEM((chunks, HPC * DH, DH), f32),
            pltpu.VMEM((chunks, half, DH), f32),
            pltpu.VMEM((chunks, half, DH), f32),
            pltpu.VMEM((chunks, slc, DH), f32),
            pltpu.VMEM((nz, PIECE, DH), f32),
            pltpu.VMEM((nz, PIECE, DH), f32),
            pltpu.VMEM((chunks, slc, DH), f32),
            pltpu.VMEM((chunks, half, DH), f32),
            pltpu.VMEM((chunks, HPC * DH, DH), f32),
            dma((3, chunks)), dma,
            dma((chunks,)), dma((chunks,)),
            dma((chunks,)), dma((chunks,)),
            dma((chunks,)), dma,
            dma, dma((chunks,)),
            dma((chunks,)), dma((chunks,)),
            dma((chunks,)), dma((chunks,)),
        ],
        compiler_params=pltpu.CompilerParams(collective_id=0, has_side_effects=True, vmem_limit_bytes=48 * 1024 * 1024),
        name="prefix_attention",
    )(
        query_feat.reshape(tokens, width),
        key_feat.reshape(tokens, width),
        value_feat.reshape(tokens, width),
        norm_gain,
    )
    return out.reshape(query_feat.shape)


def solution(mesh):
    placed = (
        P("grp", "seq", None, "head"),
        P("grp", "seq", None, "head"),
        P("grp", "seq", None, "head"),
        P("head"),
    )
    return jax.shard_map(
        per_device,
        mesh=mesh,
        in_specs=placed,
        out_specs=P("grp", "seq", None, "head"),
        check_vma=False,
    )
```

time: 185 us -> 52 us (0.28)
  the two profiles are of different devices: /device:TPU:2 before, /device:TPU:1 now
where the time goes in v1:
time: 52 us; the launch traced here: 51.7 us
  Pallas kernels  46.7 us (90%)
  local copies, waits for them, and re-layouts  4.97 us (10%)
    pallas_call x1, Pallas kernels, per_device(): pl.pallas_call(kernel, out_shape=jax.ShapeDtypeStruct((tokens, width), jn...  46.7 us
    unnamed x9, local copies, waits for them, and re-layouts  4.97 us

profile of v1, /device:TPU:1, one launch (start us, length us, event | category | flops | bytes accessed | tf_op | source)
XLA Modules:
  0.0 51.7 jit_solution(15113206356326753682)
XLA Ops:
  0.0 0.0 copy-start.3
  0.0 0.7 %copy-done.3 = f32[768]{0:T(1024)S(1)} copy-done((f32[768]{0:T(1024)S(1)}, f32[768]{0:T(1024)}, u32[]{:S(2)}) %copy-start.3) | copy-done | bytes 3096
  0.7 0.0 copy-start
  0.7 1.1 %copy-done = bf16[1,1,512,768]{3,2,1,0:T(8,128)(2,1)S(1)} copy-done((bf16[1,1,512,768]{3,2,1,0:T(8,128)(2,1)S(1)}, bf16[1,1,512,768]{3,2,1,0:T(8,128)(2,1)}, u32[]{:S(2)}) %copy-start) | copy-done | bytes 786456
  1.8 0.0 copy-start.1
  1.8 1.1 %copy-done.1 = bf16[1,1,512,768]{3,2,1,0:T(8,128)(2,1)S(1)} copy-done((bf16[1,1,512,768]{3,2,1,0:T(8,128)(2,1)S(1)}, bf16[1,1,512,768]{3,2,1,0:T(8,128)(2,1)}, u32[]{:S(2)}) %copy-start.1) | copy-done | bytes 786456
  3.0 0.0 copy-start.2
  3.0 1.1 %copy-done.2 = bf16[1,1,512,768]{3,2,1,0:T(8,128)(2,1)S(1)} copy-done((bf16[1,1,512,768]{3,2,1,0:T(8,128)(2,1)S(1)}, bf16[1,1,512,768]{3,2,1,0:T(8,128)(2,1)}, u32[]{:S(2)}) %copy-start.2) | copy-done | bytes 786456
  4.1 46.7 %prefix_attention.1 = bf16[512,768]{1,0:T(8,128)(2,1)S(1)} custom-call(bf16[512,768]{1,0:T(8,128)(2,1)S(1)} %bitcast.5, bf16[512,768]{1,0:T(8,128)(2,1)S(1)} %bitcast.6, bf16[512,768]{1,0:T(8,128)(2,1)S(1)} %bitcast.7, f32[768]{0:T(1024)S(1)} %copy-done.3), custom_call_target="tpu_custom_call" | custom-call | tf_op jit(solution)/shard_map/prefix_attention/pallas_call | solution.py:220
  50.8 0.9 %copy.6 = bf16[1,1,512,768]{3,2,1,0:T(8,128)(2,1)} copy(bf16[1,1,512,768]{3,2,1,0:T(8,128)(2,1)S(1)} %bitcast.4) | data formatting | bytes 1572864
Async XLA Ops:
  0.0 0.7 %copy-start.3 = (f32[768]{0:T(1024)S(1)}, f32[768]{0:T(1024)}, u32[]{:S(2)}) copy-start(f32[768]{0:T(1024)} %refs_3_.1) | copy-start | bytes 9220
  0.7 1.1 %copy-start = (bf16[1,1,512,768]{3,2,1,0:T(8,128)(2,1)S(1)}, bf16[1,1,512,768]{3,2,1,0:T(8,128)(2,1)}, u32[]{:S(2)}) copy-start(bf16[1,1,512,768]{3,2,1,0:T(8,128)(2,1)} %param.4) | copy-start | bytes 2359300
  1.8 1.1 %copy-start.1 = (bf16[1,1,512,768]{3,2,1,0:T(8,128)(2,1)S(1)}, bf16[1,1,512,768]{3,2,1,0:T(8,128)(2,1)}, u32[]{:S(2)}) copy-start(bf16[1,1,512,768]{3,2,1,0:T(8,128)(2,1)} %param.5) | copy-start | bytes 2359300
  3.0 1.1 %copy-start.2 = (bf16[1,1,512,768]{3,2,1,0:T(8,128)(2,1)S(1)}, bf16[1,1,512,768]{3,2,1,0:T(8,128)(2,1)}, u32[]{:S(2)}) copy-start(bf16[1,1,512,768]{3,2,1,0:T(8,128)(2,1)} %param.6) | copy-start | bytes 2359300

commit v2 on v1

v2 whole, which is shorter than its diff:
```python
import jax
import jax.numpy as jnp
from jax import lax
from jax.experimental import pallas as pl
from jax.experimental.pallas import tpu as pltpu
from jax.sharding import PartitionSpec as P

DH = 128
MESH = pl.DeviceIdType.MESH
HPC = 2
REACH = 4


def take(sem, ref):
    pltpu.make_async_copy(ref, ref, sem).wait()


def body(nx, nz, eps, q_hbm, k_hbm, v_hbm, gain_hbm, out_ref, qb, kb, vb, gain, mixed,
         kv, pk, ts, ra, gs, rw, run, cs, rf,
         in_sem, gain_sem, sc, rc, sa, rcv_a, s1, r1, s3, r3, s4, r4):
    seq, z = lax.axis_index("seq"), lax.axis_index("grp")
    core, x = lax.rem(seq, 2), seq // 2
    tokens, width = qb.shape
    chunks = width // (HPC * DH)
    half = DH
    slc = half // nx
    rows = tokens // 2
    first = jnp.logical_and(jnp.logical_and(seq == 0, z == 0), lax.axis_index("head") == 0)

    def chip(dx):
        return {"seq": lax.rem(x + dx, nx) * 2 + core}

    def along(dz):
        return {"grp": lax.rem(z + dz, nz)}

    partner = {"seq": x * 2 + 1 - core}

    def remote(src, dst, send, recv, where):
        pltpu.make_async_remote_copy(
            src_ref=src, dst_ref=dst, send_sem=send, recv_sem=recv, device_id=where, device_id_type=MESH
        ).start()

    barrier = pltpu.get_barrier_semaphore()
    pl.semaphore_signal(barrier, inc=1, device_id=partner, device_id_type=MESH)
    for dx in range(1, nx):
        pl.semaphore_signal(barrier, inc=1, device_id=chip(dx), device_id_type=MESH)
    for d in range(1, REACH + 1):
        @pl.when(z >= d)
        def _():
            pl.semaphore_signal(barrier, inc=1, device_id={"grp": z - d}, device_id_type=MESH)

    def greeted():
        pl.semaphore_wait(barrier, 1 + nx - 1 + jnp.minimum(REACH, nz - 1 - z))

    loads = []
    for i, (hbm, buf) in enumerate(((k_hbm, kb), (v_hbm, vb), (q_hbm, qb))):
        for n in range(chunks):
            cols = pl.ds(n * HPC * DH, HPC * DH)
            loads.append(pltpu.make_async_copy(hbm.at[:, cols], buf.at[:, cols], in_sem.at[i, n]))
    for n in range(chunks):
        loads[n].start()
        loads[chunks + n].start()
    for n in range(chunks):
        loads[2 * chunks + n].start()
    gain_load = pltpu.make_async_copy(gain_hbm, gain, gain_sem)
    gain_load.start()

    def head(h):
        return pl.ds(h * DH, DH)

    later = lax.broadcasted_iota(jnp.int32, (rows, rows), 0) >= lax.broadcasted_iota(jnp.int32, (rows, rows), 1)

    def local_attention(h):
        cut = head(h)
        for r in range(2):
            part = pl.ds(r * rows, rows)
            qr = qb[part, cut]
            own_scores = lax.dot_general(qr, kb[part, cut], (((1,), (1,)), ((), ())), preferred_element_type=jnp.float32)
            weights = jnp.where(later, own_scores, 0.0).astype(jnp.bfloat16)
            acc = jnp.dot(weights, vb[part, cut], preferred_element_type=jnp.float32)
            if r == 1:
                first = pl.ds(0, rows)
                full = lax.dot_general(qr, kb[first, cut], (((1,), (1,)), ((), ())), preferred_element_type=jnp.float32)
                acc = acc + jnp.dot(full.astype(jnp.bfloat16), vb[first, cut], preferred_element_type=jnp.float32)
            mixed[part, cut] = acc

    def attend():
        for n in range(chunks):
            for j in range(HPC):
                local_attention(n * HPC + j)

    def exchange(n):
        remote(kv.at[n], pk.at[n], sc.at[n], rc.at[n], partner)

    @pl.when(first)
    def _():
        greeted()

    for n in range(chunks):
        loads[n].wait()
        loads[chunks + n].wait()
        for j in range(HPC):
            h = n * HPC + j
            kv[n, pl.ds(j * DH, DH), :] = lax.dot_general(
                kb[:, head(h)], vb[:, head(h)], (((0,), (0,)), ((), ())), preferred_element_type=jnp.float32
            )

        @pl.when(first)
        def _():
            exchange(n)

    for n in range(chunks):
        loads[2 * chunks + n].wait()
    gain_load.wait()
    for d in range(1, REACH + 1):
        @pl.when(z < d)
        def _():
            for n in range(chunks):
                rw[n, d - 1] = jnp.zeros((slc, DH), jnp.float32)

    @pl.when(jnp.logical_not(first))
    def _():
        attend()
        greeted()
        for n in range(chunks):
            exchange(n)

    mine = pl.ds(core * half, half)
    for n in range(chunks):
        take(rc.at[n], pk.at[n])
        ts[n] = kv[n, mine, :] + pk[n, mine, :]
        for dx in (2, 1, 3):
            to = lax.rem(x + dx, nx)
            remote(ts.at[n, pl.ds(to * slc, slc)], ra.at[n, pl.ds(x * slc, slc)], sa.at[n], rcv_a.at[n], chip(dx))
        ra[n, pl.ds(x * slc, slc), :] = ts[n, pl.ds(x * slc, slc), :]

    for n in range(chunks):
        take(rcv_a.at[n], ra.at[n, pl.ds(0, (nx - 1) * slc)])
        total = ra[n, pl.ds(0, slc), :]
        for i in range(1, nx):
            total = total + ra[n, pl.ds(i * slc, slc), :]
        gs[n] = total
        for d in range(1, REACH):
            @pl.when(z + d < nz)
            def _():
                remote(gs.at[n], rw.at[n, d - 1], s1.at[n, d - 1], r1.at[n, d - 1], {"grp": z + d})

    for n in range(chunks):
        for d in range(1, REACH + 1):
            @pl.when(z >= d)
            def _():
                take(r1.at[n, d - 1], rw.at[n, d - 1])

        before = rw[n, REACH - 1]
        for d in range(REACH - 1, 0, -1):
            before = before + rw[n, d - 1]
        run[n] = before + gs[n]

        @pl.when(z + REACH < nz)
        def _():
            remote(run.at[n], rw.at[n, REACH - 1], s1.at[n, REACH - 1], r1.at[n, REACH - 1], {"grp": z + REACH})

        for i in range(nx):
            cs[n, pl.ds(i * slc, slc), :] = before
            before = before + ra[n, pl.ds(i * slc, slc), :]
        land = pl.ds(core * half + x * slc, slc)
        for dx in (2, 1, 3):
            to = lax.rem(x + dx, nx)
            remote(cs.at[n, pl.ds(to * slc, slc)], rf.at[n, land], s3.at[n], r3.at[n], chip(dx))
        rf[n, land, :] = cs[n, pl.ds(x * slc, slc), :]

    for n in range(chunks):
        take(r3.at[n], rf.at[n, pl.ds(0, (nx - 1) * slc)])
        remote(rf.at[n, mine], rf.at[n, mine], s4.at[n], r4.at[n], partner)

    @pl.when(first)
    def _():
        attend()

    second = core == 1
    for n in range(chunks):
        take(r4.at[n], rf.at[n, pl.ds(0, half)])
        for j in range(HPC):
            h = n * HPC + j
            at = pl.ds(j * DH, DH)
            state = rf[n, at, :] + jnp.where(second, pk[n, at, :], 0.0)
            m = mixed[:, head(h)] + jnp.dot(
                qb[:, head(h)], state.astype(jnp.bfloat16), preferred_element_type=jnp.float32
            )
            meansq = jnp.mean(m * m, axis=-1, keepdims=True)
            out_ref[:, head(h)] = (m * lax.rsqrt(meansq + eps) * gain[head(h)].reshape(1, DH)).astype(jnp.bfloat16)

    for n in range(chunks):
        take(sc.at[n], kv.at[n])
        take(sa.at[n], ts.at[n, pl.ds(0, (nx - 1) * slc)])
        take(s3.at[n], cs.at[n, pl.ds(0, (nx - 1) * slc)])
        take(s4.at[n], rf.at[n, pl.ds(0, half)])

        for d in range(1, REACH + 1):
            @pl.when(z + d < nz)
            def _():
                take(s1.at[n, d - 1], gs.at[n])


def per_device(query_feat, key_feat, value_feat, norm_gain):
    tokens, width = query_feat.shape[2:]
    nx, nz = lax.axis_size("seq") // 2, lax.axis_size("grp")
    chunks = width // (HPC * DH)
    half, slc = DH, DH // nx
    f32 = jnp.float32
    dma = pltpu.SemaphoreType.DMA

    def kernel(*refs):
        body(nx, nz, 1e-05, *refs)

    hbm = pl.BlockSpec(memory_space=pltpu.HBM)
    vmem = pl.BlockSpec(memory_space=pltpu.VMEM)
    out = pl.pallas_call(
        kernel,
        out_shape=jax.ShapeDtypeStruct((tokens, width), jnp.bfloat16),
        in_specs=[hbm, hbm, hbm, hbm],
        out_specs=vmem,
        scratch_shapes=[
            pltpu.VMEM((tokens, width), jnp.bfloat16),
            pltpu.VMEM((tokens, width), jnp.bfloat16),
            pltpu.VMEM((tokens, width), jnp.bfloat16),
            pltpu.VMEM((width,), f32),
            pltpu.VMEM((tokens, width), f32),
            pltpu.VMEM((chunks, HPC * DH, DH), f32),
            pltpu.VMEM((chunks, HPC * DH, DH), f32),
            pltpu.VMEM((chunks, half, DH), f32),
            pltpu.VMEM((chunks, half, DH), f32),
            pltpu.VMEM((chunks, slc, DH), f32),
            pltpu.VMEM((chunks, REACH, slc, DH), f32),
            pltpu.VMEM((chunks, slc, DH), f32),
            pltpu.VMEM((chunks, half, DH), f32),
            pltpu.VMEM((chunks, HPC * DH, DH), f32),
            dma((3, chunks)), dma,
            dma((chunks,)), dma((chunks,)),
            dma((chunks,)), dma((chunks,)),
            dma((chunks, REACH)), dma((chunks, REACH)),
            dma((chunks,)), dma((chunks,)),
            dma((chunks,)), dma((chunks,)),
        ],
        compiler_params=pltpu.CompilerParams(collective_id=0, has_side_effects=True, vmem_limit_bytes=48 * 1024 * 1024),
        name="prefix_attention",
    )(
        *(
            pltpu.with_memory_space_constraint(a, pltpu.HBM)
            for a in (
                query_feat.reshape(tokens, width),
                key_feat.reshape(tokens, width),
                value_feat.reshape(tokens, width),
                norm_gain,
            )
        )
    )
    return out.reshape(query_feat.shape)


def solution(mesh):
    placed = (
        P("grp", "seq", None, "head"),
        P("grp", "seq", None, "head"),
        P("grp", "seq", None, "head"),
        P("head"),
    )
    return jax.shard_map(
        per_device,
        mesh=mesh,
        in_specs=placed,
        out_specs=P("grp", "seq", None, "head"),
        check_vma=False,
    )
```

time: 52 us -> 37.7 us (0.73)
  the two profiles are of different devices: /device:TPU:1 before, /device:TPU:961 now
where the time goes in v2:
time: 37.7 us; the launch traced here: 37.5 us
  Pallas kernels  36.7 us (97%)
  local copies, waits for them, and re-layouts  0.88 us (2%)
    pallas_call x1, Pallas kernels, per_device(): pl.pallas_call(kernel, out_shape=jax.ShapeDtypeStruct((tokens, width), jn...  36.7 us
    unnamed x1, local copies, waits for them, and re-layouts  0.88 us

profile of v2, /device:TPU:961, one launch (start us, length us, event | category | flops | bytes accessed | tf_op | source)
XLA Modules:
  0.0 37.5 jit_solution(16178046263388216598)
XLA Ops:
  0.0 36.7 %prefix_attention.1 = bf16[512,768]{1,0:T(8,128)(2,1)S(1)} custom-call(bf16[512,768]{1,0:T(8,128)(2,1)} %bitcast.5, bf16[512,768]{1,0:T(8,128)(2,1)} %bitcast.6, bf16[512,768]{1,0:T(8,128)(2,1)} %bitcast.7, f32[768]{0:T(1024)} %refs_3_.1), custom_call_target="tpu_custom_call" | custom-call | tf_op jit(solution)/shard_map/prefix_attention/pallas_call | solution.py:218
  36.7 0.9 %copy.6 = bf16[1,1,512,768]{3,2,1,0:T(8,128)(2,1)} copy(bf16[1,1,512,768]{3,2,1,0:T(8,128)(2,1)S(1)} %bitcast.4) | data formatting | bytes 1572864

commit v3 on v2

--- a/solution.py
+++ b/solution.py
@@ -9,6 +9,7 @@
 MESH = pl.DeviceIdType.MESH
 HPC = 2
 REACH = 4
+STEPS = ((0, 1), (1, 2), (2, REACH))
 
 
 def take(sem, ref):
@@ -16,22 +17,30 @@
 
 
 def body(nx, nz, eps, q_hbm, k_hbm, v_hbm, gain_hbm, out_ref, qb, kb, vb, gain, mixed,
-         kv, pk, ts, ra, gs, rw, run, cs, rf,
-         in_sem, gain_sem, sc, rc, sa, rcv_a, s1, r1, s3, r3, s4, r4):
+         kv, pk, ts, ra, gs, rw, two, run, bf, lt, cs, rf,
+         in_sem, gain_sem, sc, rc, sa, rcv_a, s1, r1, s3, r3, s4, r4, sl, rl, hello, word):
     seq, z = lax.axis_index("seq"), lax.axis_index("grp")
     core, x = lax.rem(seq, 2), seq // 2
     tokens, width = qb.shape
     chunks = width // (HPC * DH)
-    half = DH
+    half = HPC * DH // 2
     slc = half // nx
     rows = tokens // 2
-    first = jnp.logical_and(jnp.logical_and(seq == 0, z == 0), lax.axis_index("head") == 0)
+    plane = lax.axis_index("head") == 0
+    late = jnp.logical_and(plane, z == 0)
+    first = jnp.logical_and(late, seq == 0)
+    origin = jnp.where(plane, 1, 0)
+    relay, end = REACH, nz - 1
+
+    middle = 2 * relay
+    split = middle + 3
+    fans = ((relay, (middle, *range(relay + 1, middle))), (middle, range(middle + 1, split)), (end, range(split, end)))
+
+    def feeds(d):
+        return jnp.logical_and(z >= origin, z + d < nz)
 
     def chip(dx):
         return {"seq": lax.rem(x + dx, nx) * 2 + core}
-
-    def along(dz):
-        return {"grp": lax.rem(z + dz, nz)}
 
     partner = {"seq": x * 2 + 1 - core}
 
@@ -44,13 +53,36 @@
     pl.semaphore_signal(barrier, inc=1, device_id=partner, device_id_type=MESH)
     for dx in range(1, nx):
         pl.semaphore_signal(barrier, inc=1, device_id=chip(dx), device_id_type=MESH)
-    for d in range(1, REACH + 1):
-        @pl.when(z >= d)
-        def _():
-            pl.semaphore_signal(barrier, inc=1, device_id={"grp": z - d}, device_id_type=MESH)
+    final = jnp.logical_and(plane, z == end)
+    for there, to in ((z >= 1, z - 1), (feeds(1), z + 1), (late, end)):
+        @pl.when(there)
+        def _():
+            pl.semaphore_signal(barrier, inc=1, device_id={"grp": to}, device_id_type=MESH)
 
     def greeted():
-        pl.semaphore_wait(barrier, 1 + nx - 1 + jnp.minimum(REACH, nz - 1 - z))
+        pl.semaphore_wait(barrier, nx + jnp.minimum(jnp.maximum(z - origin, 0), 1) + jnp.minimum(nz - 1 - z, 1) + jnp.where(final, 1, 0))
+        announce(0)
+
+        @pl.when(final)
+        def _():
+            pl.semaphore_signal(word.at[1], inc=1, device_id={"grp": 0}, device_id_type=MESH)
+
+        @pl.when(late)
+        def _():
+            pl.semaphore_signal(word.at[1], inc=1, device_id={"grp": 1}, device_id_type=MESH)
+
+    def tell(i):
+        pl.semaphore_signal(hello.at[i], inc=1, device_id={"grp": z - 1}, device_id_type=MESH)
+
+    def announce(i):
+        @pl.when(z > origin)
+        def _():
+            tell(i)
+
+    def learn(i):
+        @pl.when(z + 1 < nz)
+        def _():
+            pl.semaphore_wait(hello.at[i], 1)
 
     loads = []
     for i, (hbm, buf) in enumerate(((k_hbm, kb), (v_hbm, vb), (q_hbm, qb))):
@@ -79,9 +111,9 @@
             weights = jnp.where(later, own_scores, 0.0).astype(jnp.bfloat16)
             acc = jnp.dot(weights, vb[part, cut], preferred_element_type=jnp.float32)
             if r == 1:
-                first = pl.ds(0, rows)
-                full = lax.dot_general(qr, kb[first, cut], (((1,), (1,)), ((), ())), preferred_element_type=jnp.float32)
-                acc = acc + jnp.dot(full.astype(jnp.bfloat16), vb[first, cut], preferred_element_type=jnp.float32)
+                top = pl.ds(0, rows)
+                full = lax.dot_general(qr, kb[top, cut], (((1,), (1,)), ((), ())), preferred_element_type=jnp.float32)
+                acc = acc + jnp.dot(full.astype(jnp.bfloat16), vb[top, cut], preferred_element_type=jnp.float32)
             mixed[part, cut] = acc
 
     def attend():
@@ -112,15 +144,18 @@
     for n in range(chunks):
         loads[2 * chunks + n].wait()
     gain_load.wait()
-    for d in range(1, REACH + 1):
-        @pl.when(z < d)
+    for i, d in STEPS:
+        @pl.when(z - origin < d)
         def _():
             for n in range(chunks):
-                rw[n, d - 1] = jnp.zeros((slc, DH), jnp.float32)
+                rw[n, i] = jnp.zeros((slc, DH), jnp.float32)
+
+    @pl.when(jnp.logical_and(late, jnp.logical_not(first)))
+    def _():
+        attend()
 
     @pl.when(jnp.logical_not(first))
     def _():
-        attend()
         greeted()
         for n in range(chunks):
             exchange(n)
@@ -134,32 +169,64 @@
             remote(ts.at[n, pl.ds(to * slc, slc)], ra.at[n, pl.ds(x * slc, slc)], sa.at[n], rcv_a.at[n], chip(dx))
         ra[n, pl.ds(x * slc, slc), :] = ts[n, pl.ds(x * slc, slc), :]
 
+    @pl.when(jnp.logical_and(plane, z > split + 1))
+    def _():
+        pl.semaphore_wait(word.at[0], 1)
+
+    @pl.when(jnp.logical_and(jnp.logical_and(plane, z > split), z < end))
+    def _():
+        pl.semaphore_signal(word.at[0], inc=1, device_id={"grp": z + 1}, device_id_type=MESH)
+
+    for i in range(REACH - 2):
+        learn(i)
+        announce(i + 1)
+
     for n in range(chunks):
         take(rcv_a.at[n], ra.at[n, pl.ds(0, (nx - 1) * slc)])
         total = ra[n, pl.ds(0, slc), :]
         for i in range(1, nx):
             total = total + ra[n, pl.ds(i * slc, slc), :]
         gs[n] = total
-        for d in range(1, REACH):
-            @pl.when(z + d < nz)
-            def _():
-                remote(gs.at[n], rw.at[n, d - 1], s1.at[n, d - 1], r1.at[n, d - 1], {"grp": z + d})
-
-    for n in range(chunks):
-        for d in range(1, REACH + 1):
-            @pl.when(z >= d)
-            def _():
-                take(r1.at[n, d - 1], rw.at[n, d - 1])
-
-        before = rw[n, REACH - 1]
-        for d in range(REACH - 1, 0, -1):
-            before = before + rw[n, d - 1]
-        run[n] = before + gs[n]
-
-        @pl.when(z + REACH < nz)
-        def _():
-            remote(run.at[n], rw.at[n, REACH - 1], s1.at[n, REACH - 1], r1.at[n, REACH - 1], {"grp": z + REACH})
-
+        @pl.when(feeds(1))
+        def _():
+            remote(gs.at[n], rw.at[n, 0], s1.at[n, 0], r1.at[n, 0], {"grp": z + 1})
+
+        @pl.when(late)
+        def _():
+            if n == 0:
+                pl.semaphore_wait(word.at[1], 1)
+            for i, to in enumerate((relay, 1, end, *range(2, relay))):
+                remote(gs.at[n], lt.at[n], sl.at[n, i], rl.at[n], {"grp": to})
+
+
+    def pass_on(n, source, targets):
+        @pl.when(z == source)
+        def _():
+            for i, to in enumerate(targets):
+                remote(lt.at[n], lt.at[n], sl.at[n, i], rl.at[n], {"grp": to})
+
+    @pl.when(final)
+    def _():
+        for n in range(chunks):
+            take(rl.at[n], lt.at[n])
+            pass_on(n, *fans[-1])
+
+    for n in range(chunks):
+        @pl.when(z - origin >= 1)
+        def _():
+            take(r1.at[n, 0], rw.at[n, 0])
+
+        two[n] = gs[n] + rw[n, 0]
+
+        @pl.when(feeds(2))
+        def _():
+            remote(two.at[n], rw.at[n, 1], s1.at[n, 1], r1.at[n, 1], {"grp": z + 2})
+
+    @pl.when(jnp.logical_not(late))
+    def _():
+        attend()
+
+    def hand_back(n, before):
         for i in range(nx):
             cs[n, pl.ds(i * slc, slc), :] = before
             before = before + ra[n, pl.ds(i * slc, slc), :]
@@ -168,6 +235,48 @@
             to = lax.rem(x + dx, nx)
             remote(cs.at[n, pl.ds(to * slc, slc)], rf.at[n, land], s3.at[n], r3.at[n], chip(dx))
         rf[n, land, :] = cs[n, pl.ds(x * slc, slc), :]
+
+    for n in range(chunks):
+        for i, d in STEPS[1:]:
+            @pl.when(z - origin >= d)
+            def _():
+                take(r1.at[n, i], rw.at[n, i])
+
+        before = rw[n, 2] + rw[n, 1] + rw[n, 0]
+        run[n] = before + gs[n]
+        if n == 0:
+            learn(REACH - 2)
+
+        @pl.when(feeds(REACH))
+        def _():
+            remote(run.at[n], rw.at[n, 2], s1.at[n, 2], r1.at[n, 2], {"grp": z + REACH})
+
+        bf[n] = before
+
+        @pl.when(jnp.logical_not(plane))
+        def _():
+            hand_back(n, bf[n])
+
+    @pl.when(plane)
+    def _():
+        @pl.when(z == 1)
+        def _():
+            pl.semaphore_wait(word.at[1], 1)
+            for i in range(REACH - 1):
+                tell(i)
+
+        for n in range(chunks):
+            @pl.when(jnp.logical_and(z >= 1, z < end))
+            def _():
+                take(rl.at[n], lt.at[n])
+                for source, targets in fans[:-1]:
+                    pass_on(n, source, targets)
+
+            @pl.when(z >= 1)
+            def _():
+                bf[n] = bf[n] + lt[n]
+
+            hand_back(n, bf[n])
 
     for n in range(chunks):
         take(r3.at[n], rf.at[n, pl.ds(0, (nx - 1) * slc)])
@@ -196,17 +305,29 @@
         take(s3.at[n], cs.at[n, pl.ds(0, (nx - 1) * slc)])
         take(s4.at[n], rf.at[n, pl.ds(0, half)])
 
-        for d in range(1, REACH + 1):
-            @pl.when(z + d < nz)
+        for i, d in STEPS:
+            @pl.when(feeds(d))
             def _():
-                take(s1.at[n, d - 1], gs.at[n])
+                take(s1.at[n, i], gs.at[n])
+
+        @pl.when(late)
+        def _():
+            for i in range(relay + 1):
+                take(sl.at[n, i], lt.at[n])
+
+        for source, targets in fans:
+            @pl.when(jnp.logical_and(plane, z == source))
+            def _():
+                for i in range(len(targets)):
+                    take(sl.at[n, i], lt.at[n])
 
 
 def per_device(query_feat, key_feat, value_feat, norm_gain):
     tokens, width = query_feat.shape[2:]
     nx, nz = lax.axis_size("seq") // 2, lax.axis_size("grp")
     chunks = width // (HPC * DH)
-    half, slc = DH, DH // nx
+    half = HPC * DH // 2
+    slc = half // nx
     f32 = jnp.float32
     dma = pltpu.SemaphoreType.DMA
 
@@ -231,16 +352,22 @@
             pltpu.VMEM((chunks, half, DH), f32),
             pltpu.VMEM((chunks, half, DH), f32),
             pltpu.VMEM((chunks, slc, DH), f32),
-            pltpu.VMEM((chunks, REACH, slc, DH), f32),
+            pltpu.VMEM((chunks, len(STEPS), slc, DH), f32),
+            pltpu.VMEM((chunks, slc, DH), f32),
+            pltpu.VMEM((chunks, slc, DH), f32),
+            pltpu.VMEM((chunks, slc, DH), f32),
             pltpu.VMEM((chunks, slc, DH), f32),
             pltpu.VMEM((chunks, half, DH), f32),
             pltpu.VMEM((chunks, HPC * DH, DH), f32),
             dma((3, chunks)), dma,
             dma((chunks,)), dma((chunks,)),
             dma((chunks,)), dma((chunks,)),
-            dma((chunks, REACH)), dma((chunks, REACH)),
+            dma((chunks, len(STEPS))), dma((chunks, len(STEPS))),
             dma((chunks,)), dma((chunks,)),
             dma((chunks,)), dma((chunks,)),
+            dma((chunks, nz)), dma((chunks,)),
+            pltpu.SemaphoreType.REGULAR((REACH - 1,)),
+            pltpu.SemaphoreType.REGULAR((2,)),
         ],
         compiler_params=pltpu.CompilerParams(collective_id=0, has_side_effects=True, vmem_limit_bytes=48 * 1024 * 1024),
         name="prefix_attention",

time: 37.7 us -> 31.6 us (0.84)
  the two profiles are of different devices: /device:TPU:961 before, /device:TPU:65 now
where the time goes in v3:
time: 31.6 us; the launch traced here: 31.4 us
  Pallas kernels  30.5 us (97%)
  local copies, waits for them, and re-layouts  0.88 us (3%)
    pallas_call x1, Pallas kernels, per_device(): pl.pallas_call(kernel, out_shape=jax.ShapeDtypeStruct((tokens, width), jn...  30.5 us
    unnamed x1, local copies, waits for them, and re-layouts  0.88 us

profile of v3, /device:TPU:65, one launch (start us, length us, event | category | flops | bytes accessed | tf_op | source)
XLA Modules:
  0.0 31.4 jit_solution(10314301827803330640)
XLA Ops:
  0.0 30.5 %prefix_attention.1 = bf16[512,768]{1,0:T(8,128)(2,1)S(1)} custom-call(bf16[512,768]{1,0:T(8,128)(2,1)} %bitcast.5, bf16[512,768]{1,0:T(8,128)(2,1)} %bitcast.6, bf16[512,768]{1,0:T(8,128)(2,1)} %bitcast.7, f32[768]{0:T(1024)} %refs_3_.1), custom_call_target="tpu_custom_call" | custom-call | tf_op jit(solution)/shard_map/prefix_attention/pallas_call | solution.py:339
  30.5 0.9 %copy.6 = bf16[1,1,512,768]{3,2,1,0:T(8,128)(2,1)} copy(bf16[1,1,512,768]{3,2,1,0:T(8,128)(2,1)S(1)} %bitcast.4) | data formatting | bytes 1572864

commit v4 on v3

--- a/solution.py
+++ b/solution.py
@@ -9,7 +9,7 @@
 MESH = pl.DeviceIdType.MESH
 HPC = 2
 REACH = 4
-STEPS = ((0, 1), (1, 2), (2, REACH))
+FILL = (0, 2, 4, 6)
 
 
 def take(sem, ref):
@@ -17,8 +17,8 @@
 
 
 def body(nx, nz, eps, q_hbm, k_hbm, v_hbm, gain_hbm, out_ref, qb, kb, vb, gain, mixed,
-         kv, pk, ts, ra, gs, rw, two, run, bf, lt, cs, rf,
-         in_sem, gain_sem, sc, rc, sa, rcv_a, s1, r1, s3, r3, s4, r4, sl, rl, hello, word):
+         kv, pk, ts, ra, gs, rw, run, bf, lt, lk, cs, rf,
+         in_sem, gain_sem, sc, rc, sa, rcv_a, s1, r1, s3, r3, s4, r4, sl, rl, sk, rk, hello, word, enter):
     seq, z = lax.axis_index("seq"), lax.axis_index("grp")
     core, x = lax.rem(seq, 2), seq // 2
     tokens, width = qb.shape
@@ -29,12 +29,22 @@
     plane = lax.axis_index("head") == 0
     late = jnp.logical_and(plane, z == 0)
     first = jnp.logical_and(late, seq == 0)
+    mate = jnp.logical_and(late, seq == 1)
+    others = jnp.logical_and(late, seq > 1)
+    row, odd = jnp.logical_and(others, core == 0), jnp.logical_and(others, core == 1)
     origin = jnp.where(plane, 1, 0)
     relay, end = REACH, nz - 1
+    final = jnp.logical_and(plane, z == end)
 
     middle = 2 * relay
     split = middle + 3
     fans = ((relay, (middle, *range(relay + 1, middle))), (middle, range(middle + 1, split)), (end, range(split, end)))
+
+    place = lax.rem(z, REACH)
+    tail = place == REACH - 1
+
+    def inside(d):
+        return jnp.logical_and(feeds(d), place + d < REACH)
 
     def feeds(d):
         return jnp.logical_and(z >= origin, z + d < nz)
@@ -51,38 +61,45 @@
 
     barrier = pltpu.get_barrier_semaphore()
     pl.semaphore_signal(barrier, inc=1, device_id=partner, device_id_type=MESH)
-    for dx in range(1, nx):
-        pl.semaphore_signal(barrier, inc=1, device_id=chip(dx), device_id_type=MESH)
-    final = jnp.logical_and(plane, z == end)
-    for there, to in ((z >= 1, z - 1), (feeds(1), z + 1), (late, end)):
+
+    @pl.when(jnp.logical_not(first))
+    def _():
+        for dx in range(1, nx):
+            pl.semaphore_signal(barrier, inc=1, device_id=chip(dx), device_id_type=MESH)
+
+    notes = [(feeds(d), z + d) for d in range(1, REACH + 1)]
+    @pl.when(odd)
+    def _():
+        pl.semaphore_signal(barrier, inc=1, device_id={"seq": 0}, device_id_type=MESH)
+
+    notes += [(jnp.logical_and(plane, jnp.logical_and(z >= 1, z <= relay)), 0), (late, end)]
+    for there, to in notes:
         @pl.when(there)
         def _():
             pl.semaphore_signal(barrier, inc=1, device_id={"grp": to}, device_id_type=MESH)
 
     def greeted():
-        pl.semaphore_wait(barrier, nx + jnp.minimum(jnp.maximum(z - origin, 0), 1) + jnp.minimum(nz - 1 - z, 1) + jnp.where(final, 1, 0))
-        announce(0)
+        behind = jnp.minimum(jnp.maximum(z - origin, 0), REACH)
+        behind = behind + jnp.where(first, nx - 1, 0) - jnp.where(row, 1, 0)
+        pl.semaphore_wait(barrier, nx + behind + jnp.where(late, relay, 0) + jnp.where(final, 1, 0))
+        for d in range(1, REACH + 1):
+            @pl.when(z - d >= origin)
+            def _():
+                pl.semaphore_signal(hello.at[d - 1], inc=1, device_id={"grp": z - d}, device_id_type=MESH)
 
         @pl.when(final)
         def _():
-            pl.semaphore_signal(word.at[1], inc=1, device_id={"grp": 0}, device_id_type=MESH)
-
-        @pl.when(late)
-        def _():
-            pl.semaphore_signal(word.at[1], inc=1, device_id={"grp": 1}, device_id_type=MESH)
-
-    def tell(i):
-        pl.semaphore_signal(hello.at[i], inc=1, device_id={"grp": z - 1}, device_id_type=MESH)
-
-    def announce(i):
-        @pl.when(z > origin)
-        def _():
-            tell(i)
-
-    def learn(i):
-        @pl.when(z + 1 < nz)
-        def _():
-            pl.semaphore_wait(hello.at[i], 1)
+            pl.semaphore_signal(word, inc=1, device_id={"grp": 0}, device_id_type=MESH)
+
+        @pl.when(first)
+        def _():
+            for i in range(1, nx):
+                pl.semaphore_signal(enter, inc=1, device_id={"seq": 2 * i}, device_id_type=MESH)
+
+    def learn(d, wanted):
+        @pl.when(jnp.logical_and(feeds(d), wanted))
+        def _():
+            pl.semaphore_wait(hello.at[d - 1], 1)
 
     loads = []
     for i, (hbm, buf) in enumerate(((k_hbm, kb), (v_hbm, vb), (q_hbm, qb))):
@@ -103,7 +120,7 @@
     later = lax.broadcasted_iota(jnp.int32, (rows, rows), 0) >= lax.broadcasted_iota(jnp.int32, (rows, rows), 1)
 
     def local_attention(h):
-        cut = head(h)
+        cut = pl.ds(pl.multiple_of(h * DH, DH), DH)
         for r in range(2):
             part = pl.ds(r * rows, rows)
             qr = qb[part, cut]
@@ -116,86 +133,128 @@
                 acc = acc + jnp.dot(full.astype(jnp.bfloat16), vb[top, cut], preferred_element_type=jnp.float32)
             mixed[part, cut] = acc
 
-    def attend():
-        for n in range(chunks):
-            for j in range(HPC):
-                local_attention(n * HPC + j)
+    heads_here = chunks * HPC
+
+    def attend(start=0, stop=heads_here):
+        @pl.loop(start, stop)
+        def _(h):
+            local_attention(h)
+
+    def fill(part):
+        @pl.when(jnp.logical_not(late))
+        def _():
+            attend(heads_here * FILL[part] // 6, heads_here * FILL[part + 1] // 6)
 
     def exchange(n):
         remote(kv.at[n], pk.at[n], sc.at[n], rc.at[n], partner)
 
-    @pl.when(first)
-    def _():
-        greeted()
-
-    for n in range(chunks):
+    def make(n):
         loads[n].wait()
         loads[chunks + n].wait()
+        cut = pl.ds(n * HPC * DH, HPC * DH)
+        sums = lax.dot_general(kb[:, cut], vb[:, cut], (((0,), (0,)), ((), ())), preferred_element_type=jnp.float32)
         for j in range(HPC):
-            h = n * HPC + j
-            kv[n, pl.ds(j * DH, DH), :] = lax.dot_general(
-                kb[:, head(h)], vb[:, head(h)], (((0,), (0,)), ((), ())), preferred_element_type=jnp.float32
-            )
-
-        @pl.when(first)
-        def _():
+            kv[n, pl.ds(j * DH, DH), :] = sums[j * DH:(j + 1) * DH, j * DH:(j + 1) * DH]
+
+    waits = jnp.logical_and(late, jnp.logical_not(first))
+
+    @pl.when(waits)
+    def _():
+        for n in range(chunks):
+            make(n)
+        for load in loads[2 * chunks:]:
+            load.wait()
+        attend()
+        greeted()
+        for n in range(chunks):
             exchange(n)
 
-    for n in range(chunks):
-        loads[2 * chunks + n].wait()
+    @pl.when(jnp.logical_not(waits))
+    def _():
+        for n in range(chunks):
+            if n == 0:
+                @pl.when(first)
+                def _():
+                    greeted()
+
+            make(n)
+            if n == 0:
+                @pl.when(jnp.logical_not(first))
+                def _():
+                    greeted()
+
+            @pl.when(first)
+            def _():
+                for i in range(nx):
+                    remote(kv.at[n, pl.ds(half + i * slc, slc)], lk.at[n], sk.at[n, i], rk.at[n], {"seq": 2 * i + 1})
+
+            exchange(n)
+        for load in loads[2 * chunks:]:
+            load.wait()
+
     gain_load.wait()
-    for i, d in STEPS:
-        @pl.when(z - origin < d)
+    def arrives(d):
+        return jnp.logical_and(place >= d, z - d >= origin)
+
+    for i, full in (*((d - 1, arrives(d)) for d in range(1, REACH)), (REACH - 1, z >= REACH)):
+        @pl.when(jnp.logical_not(full))
         def _():
             for n in range(chunks):
                 rw[n, i] = jnp.zeros((slc, DH), jnp.float32)
 
-    @pl.when(jnp.logical_and(late, jnp.logical_not(first)))
-    def _():
-        attend()
-
-    @pl.when(jnp.logical_not(first))
-    def _():
-        greeted()
-        for n in range(chunks):
-            exchange(n)
-
     mine = pl.ds(core * half, half)
     for n in range(chunks):
-        take(rc.at[n], pk.at[n])
-        ts[n] = kv[n, mine, :] + pk[n, mine, :]
+        @pl.when(mate)
+        def _():
+            ts[n] = kv[n, mine, :]
+
+        @pl.when(jnp.logical_not(mate))
+        def _():
+            take(rc.at[n], pk.at[n])
+            ts[n] = kv[n, mine, :] + pk[n, mine, :]
+
         for dx in (2, 1, 3):
             to = lax.rem(x + dx, nx)
-            remote(ts.at[n, pl.ds(to * slc, slc)], ra.at[n, pl.ds(x * slc, slc)], sa.at[n], rcv_a.at[n], chip(dx))
+
+            @pl.when(jnp.logical_not(jnp.logical_and(row, to == 0)))
+            def _():
+                remote(ts.at[n, pl.ds(to * slc, slc)], ra.at[n, pl.ds(x * slc, slc)], sa.at[n], rcv_a.at[n], chip(dx))
+
         ra[n, pl.ds(x * slc, slc), :] = ts[n, pl.ds(x * slc, slc), :]
 
-    @pl.when(jnp.logical_and(plane, z > split + 1))
-    def _():
-        pl.semaphore_wait(word.at[0], 1)
-
-    @pl.when(jnp.logical_and(jnp.logical_and(plane, z > split), z < end))
-    def _():
-        pl.semaphore_signal(word.at[0], inc=1, device_id={"grp": z + 1}, device_id_type=MESH)
-
-    for i in range(REACH - 2):
-        learn(i)
-        announce(i + 1)
+    @pl.when(row)
+    def _():
+        pl.semaphore_wait(enter, 1)
+        for n in range(chunks):
+            remote(ts.at[n, pl.ds(0, slc)], ra.at[n, pl.ds(x * slc, slc)], sa.at[n], rcv_a.at[n], {"seq": 0})
+
+    fill(0)
 
     for n in range(chunks):
         take(rcv_a.at[n], ra.at[n, pl.ds(0, (nx - 1) * slc)])
+
+        @pl.when(jnp.logical_and(late, core == 1))
+        def _():
+            take(rk.at[n], lk.at[n])
+            ra[n, pl.ds(0, slc), :] = ra[n, pl.ds(0, slc), :] + lk[n]
+
         total = ra[n, pl.ds(0, slc), :]
         for i in range(1, nx):
             total = total + ra[n, pl.ds(i * slc, slc), :]
         gs[n] = total
-        @pl.when(feeds(1))
-        def _():
-            remote(gs.at[n], rw.at[n, 0], s1.at[n, 0], r1.at[n, 0], {"grp": z + 1})
+        for d in range(1, REACH):
+            if n == 0:
+                learn(d, place + d < REACH)
+
+            @pl.when(inside(d))
+            def _():
+                remote(gs.at[n], rw.at[n, d - 1], s1.at[n, d - 1], r1.at[n, d - 1], {"grp": z + d})
 
         @pl.when(late)
         def _():
             if n == 0:
-                pl.semaphore_wait(word.at[1], 1)
-            for i, to in enumerate((relay, 1, end, *range(2, relay))):
+                pl.semaphore_wait(word, 1)
+            for i, to in enumerate((1, 2, relay, *range(3, relay), end)):
                 remote(gs.at[n], lt.at[n], sl.at[n, i], rl.at[n], {"grp": to})
 
 
@@ -211,20 +270,8 @@
             take(rl.at[n], lt.at[n])
             pass_on(n, *fans[-1])
 
-    for n in range(chunks):
-        @pl.when(z - origin >= 1)
-        def _():
-            take(r1.at[n, 0], rw.at[n, 0])
-
-        two[n] = gs[n] + rw[n, 0]
-
-        @pl.when(feeds(2))
-        def _():
-            remote(two.at[n], rw.at[n, 1], s1.at[n, 1], r1.at[n, 1], {"grp": z + 2})
-
-    @pl.when(jnp.logical_not(late))
-    def _():
-        attend()
+    fill(1)
+
 
     def hand_back(n, before):
         for i in range(nx):
@@ -237,19 +284,26 @@
         rf[n, land, :] = cs[n, pl.ds(x * slc, slc), :]
 
     for n in range(chunks):
-        for i, d in STEPS[1:]:
-            @pl.when(z - origin >= d)
-            def _():
-                take(r1.at[n, i], rw.at[n, i])
-
-        before = rw[n, 2] + rw[n, 1] + rw[n, 0]
+        for d in range(1, REACH):
+            @pl.when(arrives(d))
+            def _():
+                take(r1.at[n, d - 1], rw.at[n, d - 1])
+
+        near = rw[n, 0] + rw[n, 1] + rw[n, 2]
+
+        @pl.when(z >= REACH)
+        def _():
+            take(r1.at[n, REACH - 1], rw.at[n, REACH - 1])
+
+        before = rw[n, REACH - 1] + near
         run[n] = before + gs[n]
-        if n == 0:
-            learn(REACH - 2)
-
-        @pl.when(feeds(REACH))
-        def _():
-            remote(run.at[n], rw.at[n, 2], s1.at[n, 2], r1.at[n, 2], {"grp": z + REACH})
+        for d in (REACH, *range(1, REACH)):
+            if n == 0:
+                learn(d, tail)
+
+            @pl.when(jnp.logical_and(feeds(d), tail))
+            def _():
+                remote(run.at[n], rw.at[n, REACH - 1], s1.at[n, d - 1], r1.at[n, REACH - 1], {"grp": z + d})
 
         bf[n] = before
 
@@ -257,14 +311,11 @@
         def _():
             hand_back(n, bf[n])
 
+    for d in range(1, REACH + 1):
+        learn(d, jnp.logical_and(place + d >= REACH, jnp.logical_not(tail)))
+
     @pl.when(plane)
     def _():
-        @pl.when(z == 1)
-        def _():
-            pl.semaphore_wait(word.at[1], 1)
-            for i in range(REACH - 1):
-                tell(i)
-
         for n in range(chunks):
             @pl.when(jnp.logical_and(z >= 1, z < end))
             def _():
@@ -278,6 +329,7 @@
 
             hand_back(n, bf[n])
 
+    fill(2)
     for n in range(chunks):
         take(r3.at[n], rf.at[n, pl.ds(0, (nx - 1) * slc)])
         remote(rf.at[n, mine], rf.at[n, mine], s4.at[n], r4.at[n], partner)
@@ -285,6 +337,11 @@
     @pl.when(first)
     def _():
         attend()
+
+    @pl.when(mate)
+    def _():
+        for n in range(chunks):
+            take(rc.at[n], pk.at[n])
 
     second = core == 1
     for n in range(chunks):
@@ -305,10 +362,15 @@
         take(s3.at[n], cs.at[n, pl.ds(0, (nx - 1) * slc)])
         take(s4.at[n], rf.at[n, pl.ds(0, half)])
 
-        for i, d in STEPS:
-            @pl.when(feeds(d))
-            def _():
-                take(s1.at[n, i], gs.at[n])
+        for d in range(1, REACH + 1):
+            @pl.when(jnp.logical_and(feeds(d), jnp.logical_or(tail, place + d < REACH)))
+            def _():
+                take(s1.at[n, d - 1], gs.at[n])
+
+        @pl.when(first)
+        def _():
+            for i in range(nx):
+                take(sk.at[n, i], lk.at[n])
 
         @pl.when(late)
         def _():
@@ -352,7 +414,7 @@
             pltpu.VMEM((chunks, half, DH), f32),
             pltpu.VMEM((chunks, half, DH), f32),
             pltpu.VMEM((chunks, slc, DH), f32),
-            pltpu.VMEM((chunks, len(STEPS), slc, DH), f32),
+            pltpu.VMEM((chunks, REACH, slc, DH), f32),
             pltpu.VMEM((chunks, slc, DH), f32),
             pltpu.VMEM((chunks, slc, DH), f32),
             pltpu.VMEM((chunks, slc, DH), f32),
@@ -362,12 +424,14 @@
             dma((3, chunks)), dma,
             dma((chunks,)), dma((chunks,)),
             dma((chunks,)), dma((chunks,)),
-            dma((chunks, len(STEPS))), dma((chunks, len(STEPS))),
+            dma((chunks, REACH)), dma((chunks, REACH)),
             dma((chunks,)), dma((chunks,)),
             dma((chunks,)), dma((chunks,)),
             dma((chunks, nz)), dma((chunks,)),
-            pltpu.SemaphoreType.REGULAR((REACH - 1,)),
-            pltpu.SemaphoreType.REGULAR((2,)),
+            dma((chunks, nx)), dma((chunks,)),
+            pltpu.SemaphoreType.REGULAR((REACH,)),
+            pltpu.SemaphoreType.REGULAR,
+            pltpu.SemaphoreType.REGULAR,
         ],
         compiler_params=pltpu.CompilerParams(collective_id=0, has_side_effects=True, vmem_limit_bytes=48 * 1024 * 1024),
         name="prefix_attention",

time: 31.6 us -> 31.2 us (0.987)
    pallas_call x1, Pallas kernels: 30.5 us -> 30.2 us  [per_device(): pl.pallas_call(kernel, out_shape=jax.ShapeDtypeStruct((tokens, width), jn...]
where the time goes in v4:
time: 31.2 us; the launch traced here: 31.1 us
  Pallas kernels  30.2 us (97%)
  local copies, waits for them, and re-layouts  0.88 us (3%)
    pallas_call x1, Pallas kernels, per_device(): pl.pallas_call(kernel, out_shape=jax.ShapeDtypeStruct((tokens, width), jn...  30.2 us
    unnamed x1, local copies, waits for them, and re-layouts  0.88 us

profile of v4, /device:TPU:65, one launch (start us, length us, event | category | flops | bytes accessed | tf_op | source)
XLA Modules:
  0.0 31.1 jit_solution(7715181026191486556)
XLA Ops:
  0.0 30.2 %prefix_attention.1 = bf16[512,768]{1,0:T(8,128)(2,1)S(1)} custom-call(bf16[512,768]{1,0:T(8,128)(2,1)} %bitcast.5, bf16[512,768]{1,0:T(8,128)(2,1)} %bitcast.6, bf16[512,768]{1,0:T(8,128)(2,1)} %bitcast.7, f32[768]{0:T(1024)} %refs_3_.1), custom_call_target="tpu_custom_call" | custom-call | tf_op jit(solution)/shard_map/prefix_attention/pallas_call | solution.py:401
  30.2 0.9 %copy.6 = bf16[1,1,512,768]{3,2,1,0:T(8,128)(2,1)} copy(bf16[1,1,512,768]{3,2,1,0:T(8,128)(2,1)S(1)} %bitcast.4) | data formatting | bytes 1572864

commit v5 on v4

--- a/solution.py
+++ b/solution.py
@@ -7,7 +7,7 @@
 
 DH = 128
 MESH = pl.DeviceIdType.MESH
-HPC = 2
+HPC = 3
 REACH = 4
 FILL = (0, 2, 4, 6)
 
@@ -59,6 +59,19 @@
             src_ref=src, dst_ref=dst, send_sem=send, recv_sem=recv, device_id=where, device_id_type=MESH
         ).start()
 
+    loads = []
+    for i, (hbm, buf) in enumerate(((k_hbm, kb), (v_hbm, vb), (q_hbm, qb))):
+        for n in range(chunks):
+            cols = pl.ds(n * HPC * DH, HPC * DH)
+            loads.append(pltpu.make_async_copy(hbm.at[:, cols], buf.at[:, cols], in_sem.at[i, n]))
+    for n in range(chunks):
+        loads[n].start()
+        loads[chunks + n].start()
+    for n in range(chunks):
+        loads[2 * chunks + n].start()
+    gain_load = pltpu.make_async_copy(gain_hbm, gain, gain_sem)
+    gain_load.start()
+
     barrier = pltpu.get_barrier_semaphore()
     pl.semaphore_signal(barrier, inc=1, device_id=partner, device_id_type=MESH)
 
@@ -100,19 +113,6 @@
         @pl.when(jnp.logical_and(feeds(d), wanted))
         def _():
             pl.semaphore_wait(hello.at[d - 1], 1)
-
-    loads = []
-    for i, (hbm, buf) in enumerate(((k_hbm, kb), (v_hbm, vb), (q_hbm, qb))):
-        for n in range(chunks):
-            cols = pl.ds(n * HPC * DH, HPC * DH)
-            loads.append(pltpu.make_async_copy(hbm.at[:, cols], buf.at[:, cols], in_sem.at[i, n]))
-    for n in range(chunks):
-        loads[n].start()
-        loads[chunks + n].start()
-    for n in range(chunks):
-        loads[2 * chunks + n].start()
-    gain_load = pltpu.make_async_copy(gain_hbm, gain, gain_sem)
-    gain_load.start()
 
     def head(h):
         return pl.ds(h * DH, DH)
@@ -252,11 +252,16 @@
 
         @pl.when(late)
         def _():
-            if n == 0:
-                pl.semaphore_wait(word, 1)
-            for i, to in enumerate((1, 2, relay, *range(3, relay), end)):
+            for i, to in enumerate((1, 2, relay)):
                 remote(gs.at[n], lt.at[n], sl.at[n, i], rl.at[n], {"grp": to})
 
+
+    @pl.when(late)
+    def _():
+        pl.semaphore_wait(word, 1)
+        for n in range(chunks):
+            for i, to in enumerate((*range(3, relay), end)):
+                remote(gs.at[n], lt.at[n], sl.at[n, 3 + i], rl.at[n], {"grp": to})
 
     def pass_on(n, source, targets):
         @pl.when(z == source)
@@ -342,6 +347,32 @@
     def _():
         for n in range(chunks):
             take(rc.at[n], pk.at[n])
+
+    for n in range(chunks):
+        take(sc.at[n], kv.at[n])
+        take(sa.at[n], ts.at[n, pl.ds(0, (nx - 1) * slc)])
+        take(s3.at[n], cs.at[n, pl.ds(0, (nx - 1) * slc)])
+
+        for d in range(1, REACH + 1):
+            @pl.when(jnp.logical_and(feeds(d), jnp.logical_or(tail, place + d < REACH)))
+            def _():
+                take(s1.at[n, d - 1], gs.at[n])
+
+        @pl.when(first)
+        def _():
+            for i in range(nx):
+                take(sk.at[n, i], lk.at[n])
+
+        @pl.when(late)
+        def _():
+            for i in range(relay + 1):
+                take(sl.at[n, i], lt.at[n])
+
+        for source, targets in fans:
+            @pl.when(jnp.logical_and(plane, z == source))
+            def _():
+                for i in range(len(targets)):
+                    take(sl.at[n, i], lt.at[n])
 
     second = core == 1
     for n in range(chunks):
@@ -357,31 +388,7 @@
             out_ref[:, head(h)] = (m * lax.rsqrt(meansq + eps) * gain[head(h)].reshape(1, DH)).astype(jnp.bfloat16)
 
     for n in range(chunks):
-        take(sc.at[n], kv.at[n])
-        take(sa.at[n], ts.at[n, pl.ds(0, (nx - 1) * slc)])
-        take(s3.at[n], cs.at[n, pl.ds(0, (nx - 1) * slc)])
         take(s4.at[n], rf.at[n, pl.ds(0, half)])
-
-        for d in range(1, REACH + 1):
-            @pl.when(jnp.logical_and(feeds(d), jnp.logical_or(tail, place + d < REACH)))
-            def _():
-                take(s1.at[n, d - 1], gs.at[n])
-
-        @pl.when(first)
-        def _():
-            for i in range(nx):
-                take(sk.at[n, i], lk.at[n])
-
-        @pl.when(late)
-        def _():
-            for i in range(relay + 1):
-                take(sl.at[n, i], lt.at[n])
-
-        for source, targets in fans:
-            @pl.when(jnp.logical_and(plane, z == source))
-            def _():
-                for i in range(len(targets)):
-                    take(sl.at[n, i], lt.at[n])
 
 
 def per_device(query_feat, key_feat, value_feat, norm_gain):

time: 31.2 us -> 29.6 us (0.949)
  Pallas kernels: 30.2 us -> 28.5 us
    pallas_call x1, Pallas kernels: 30.2 us -> 28.5 us  [per_device(): pl.pallas_call(kernel, out_shape=jax.ShapeDtypeStruct((tokens, width), jn...]
where the time goes in v5:
time: 29.6 us; the launch traced here: 29.4 us
  Pallas kernels  28.5 us (96%)
  local copies, waits for them, and re-layouts  0.88 us (3%)
    pallas_call x1, Pallas kernels, per_device(): pl.pallas_call(kernel, out_shape=jax.ShapeDtypeStruct((tokens, width), jn...  28.5 us
    unnamed x1, local copies, waits for them, and re-layouts  0.88 us

profile of v5, /device:TPU:65, one launch (start us, length us, event | category | flops | bytes accessed | tf_op | source)
XLA Modules:
  0.0 29.4 jit_solution(10688966323782059033)
XLA Ops:
  0.0 28.5 %prefix_attention.1 = bf16[512,768]{1,0:T(8,128)(2,1)S(1)} custom-call(bf16[512,768]{1,0:T(8,128)(2,1)} %bitcast.5, bf16[512,768]{1,0:T(8,128)(2,1)} %bitcast.6, bf16[512,768]{1,0:T(8,128)(2,1)} %bitcast.7, f32[768]{0:T(1024)} %refs_3_.1), custom_call_target="tpu_custom_call" | custom-call | tf_op jit(solution)/shard_map/prefix_attention/pallas_call | solution.py:408
  28.5 0.9 %copy.6 = bf16[1,1,512,768]{3,2,1,0:T(8,128)(2,1)} copy(bf16[1,1,512,768]{3,2,1,0:T(8,128)(2,1)S(1)} %bitcast.4) | data formatting | bytes 1572864

commit v6 on v5

--- a/solution.py
+++ b/solution.py
@@ -151,10 +151,11 @@
     def make(n):
         loads[n].wait()
         loads[chunks + n].wait()
-        cut = pl.ds(n * HPC * DH, HPC * DH)
-        sums = lax.dot_general(kb[:, cut], vb[:, cut], (((0,), (0,)), ((), ())), preferred_element_type=jnp.float32)
         for j in range(HPC):
-            kv[n, pl.ds(j * DH, DH), :] = sums[j * DH:(j + 1) * DH, j * DH:(j + 1) * DH]
+            cut = head(n * HPC + j)
+            kv[n, pl.ds(j * DH, DH), :] = lax.dot_general(
+                kb[:, cut], vb[:, cut], (((0,), (0,)), ((), ())), preferred_element_type=jnp.float32
+            )
 
     waits = jnp.logical_and(late, jnp.logical_not(first))
 
@@ -375,17 +376,25 @@
                     take(sl.at[n, i], lt.at[n])
 
     second = core == 1
+
+    def finish(n, j):
+        cut = pl.ds(pl.multiple_of((n * HPC + j) * DH, DH), DH)
+        at = pl.ds(pl.multiple_of(j * DH, DH), DH)
+        state = rf[n, at, :] + jnp.where(second, pk[n, at, :], 0.0)
+        m = mixed[:, cut] + jnp.dot(qb[:, cut], state.astype(jnp.bfloat16), preferred_element_type=jnp.float32)
+        meansq = jnp.mean(m * m, axis=-1, keepdims=True)
+        scale = gain[head(n * HPC)]
+        for i in range(1, HPC):
+            scale = jnp.where(j == i, gain[head(n * HPC + i)], scale)
+        out_ref[:, cut] = (m * lax.rsqrt(meansq + eps) * scale.reshape(1, DH)).astype(jnp.bfloat16)
+
+    for n in range(chunks):
+        finish(n, (HPC - 1) * core)
     for n in range(chunks):
         take(r4.at[n], rf.at[n, pl.ds(0, half)])
-        for j in range(HPC):
-            h = n * HPC + j
-            at = pl.ds(j * DH, DH)
-            state = rf[n, at, :] + jnp.where(second, pk[n, at, :], 0.0)
-            m = mixed[:, head(h)] + jnp.dot(
-                qb[:, head(h)], state.astype(jnp.bfloat16), preferred_element_type=jnp.float32
-            )
-            meansq = jnp.mean(m * m, axis=-1, keepdims=True)
-            out_ref[:, head(h)] = (m * lax.rsqrt(meansq + eps) * gain[head(h)].reshape(1, DH)).astype(jnp.bfloat16)
+        for i in range(1, HPC - 1):
+            finish(n, i)
+        finish(n, (HPC - 1) * (1 - core))
 
     for n in range(chunks):
         take(s4.at[n], rf.at[n, pl.ds(0, half)])

time: 29.6 us -> 29.4 us (level)
  no operation moved by 1% of the time
where the time goes in v6:
time: 29.4 us; the launch traced here: 29.3 us
  Pallas kernels  28.4 us (97%)
  local copies, waits for them, and re-layouts  0.88 us (3%)
    pallas_call x1, Pallas kernels, per_device(): pl.pallas_call(kernel, out_shape=jax.ShapeDtypeStruct((tokens, width), jn...  28.4 us
    unnamed x1, local copies, waits for them, and re-layouts  0.88 us

profile of v6, /device:TPU:65, one launch (start us, length us, event | category | flops | bytes accessed | tf_op | source)
XLA Modules:
  0.0 29.3 jit_solution(14563593541901910784)
XLA Ops:
  0.0 28.4 %prefix_attention.1 = bf16[512,768]{1,0:T(8,128)(2,1)S(1)} custom-call(bf16[512,768]{1,0:T(8,128)(2,1)} %bitcast.5, bf16[512,768]{1,0:T(8,128)(2,1)} %bitcast.6, bf16[512,768]{1,0:T(8,128)(2,1)} %bitcast.7, f32[768]{0:T(1024)} %refs_3_.1), custom_call_target="tpu_custom_call" | custom-call | tf_op jit(solution)/shard_map/prefix_attention/pallas_call | solution.py:417
  28.4 0.9 %copy.6 = bf16[1,1,512,768]{3,2,1,0:T(8,128)(2,1)} copy(bf16[1,1,512,768]{3,2,1,0:T(8,128)(2,1)S(1)} %bitcast.4) | data formatting | bytes 1572864

commit v7 on v6

--- a/solution.py
+++ b/solution.py
@@ -186,7 +186,7 @@
 
             @pl.when(first)
             def _():
-                for i in range(nx):
+                for i in (2, 1, 3, 0):
                     remote(kv.at[n, pl.ds(half + i * slc, slc)], lk.at[n], sk.at[n, i], rk.at[n], {"seq": 2 * i + 1})
 
             exchange(n)

time: 29.4 us -> 29.2 us (level)
  Pallas kernels: 28.4 us -> 28.1 us
where the time goes in v7:
time: 29.2 us; the launch traced here: 29 us
  Pallas kernels  28.1 us (96%)
  local copies, waits for them, and re-layouts  0.88 us (3%)
    pallas_call x1, Pallas kernels, per_device(): pl.pallas_call(kernel, out_shape=jax.ShapeDtypeStruct((tokens, width), jn...  28.1 us
    unnamed x1, local copies, waits for them, and re-layouts  0.88 us

profile of v7, /device:TPU:65, one launch (start us, length us, event | category | flops | bytes accessed | tf_op | source)
XLA Modules:
  0.0 29.0 jit_solution(11339911663562603495)
XLA Ops:
  0.0 28.1 %prefix_attention.1 = bf16[512,768]{1,0:T(8,128)(2,1)S(1)} custom-call(bf16[512,768]{1,0:T(8,128)(2,1)} %bitcast.5, bf16[512,768]{1,0:T(8,128)(2,1)} %bitcast.6, bf16[512,768]{1,0:T(8,128)(2,1)} %bitcast.7, f32[768]{0:T(1024)} %refs_3_.1), custom_call_target="tpu_custom_call" | custom-call | tf_op jit(solution)/shard_map/prefix_attention/pallas_call | solution.py:417
  28.1 0.9 %copy.6 = bf16[1,1,512,768]{3,2,1,0:T(8,128)(2,1)} copy(bf16[1,1,512,768]{3,2,1,0:T(8,128)(2,1)S(1)} %bitcast.4) | data formatting | bytes 1572864
